TPU v7x, 32 devices: a whole 2x2x4 slice. The times are simulated.
32 devices in a mesh: fsdp: 2 (over x), ctx: 4 (over y, core), tp: 4 (over z).
Axes of the slice: x: 2, y: 2, z: 4, core: 2. Of those that a mesh axis runs over, the one named last changes fastest.
Arguments:
- inputs: bfloat16 [4, 16, 196, 768], P('fsdp', 'ctx', 'tp'), may hold values from -6 to 6
- cotangent: bfloat16 [4, 16, 196, 768], P('fsdp', 'ctx', 'tp'), may hold values from -6 to 6
- norm_gain: float32 [3, 768], replicated, may hold values from 0.5 to 1.5
- norm_bias: float32 [3, 768], replicated, may hold values from -1 to 1
- attn_weight: bfloat16 [2, 3, 768, 768], P(None, None, 'fsdp', 'tp'), may hold values from -0.21875 to 0.21875
- attn_bias: float32 [2, 2, 768], P(None, None, 'tp'), may hold values from -1 to 1
- out_weight: bfloat16 [2, 768, 768], P(None, 'tp', 'fsdp'), may hold values from -0.625 to 0.625
- out_bias: float32 [2, 768], replicated, may hold values from -1 to 1
- up_weight: bfloat16 [768, 3072], P('fsdp', 'tp'), may hold values from -0.21875 to 0.21875
- up_bias: float32 [3072], replicated, may hold values from -1 to 1
- down_weight: bfloat16 [3072, 768], P('tp', 'fsdp'), may hold values from -0.109375 to 0.109375
- down_bias: float32 [768], replicated, may hold values from -1 to 1
Outputs:
- outputs: bfloat16 [4, 16, 196, 768], P('fsdp', 'ctx', 'tp')
- input_grad: bfloat16 [4, 16, 196, 768], P('fsdp', 'ctx', 'tp')
- grad_norm_gain: float32 [3, 768], replicated
- grad_norm_bias: float32 [3, 768], replicated
- grad_attn_weight: float32 [2, 3, 768, 768], P(None, None, ('fsdp', 'ctx'), 'tp')
- grad_attn_bias: float32 [2, 2, 768], P(None, None, 'tp')
- grad_out_weight: float32 [2, 768, 768], P(None, 'tp', ('fsdp', 'ctx'))
- grad_out_bias: float32 [2, 768], replicated
- grad_up_weight: float32 [768, 3072], P(('fsdp', 'ctx'), 'tp')
- grad_up_bias: float32 [3072], replicated
- grad_down_weight: float32 [3072, 768], P('tp', ('fsdp', 'ctx'))
- grad_down_bias: float32 [768], replicated
All inputs are finite; a program needn't handle non-finite values.
Results may differ from a plain program's by a relative error of at most 0.025.
Values may be sent and summed in bfloat16 or wider, within the bound.
A program may use at most 128 MiB of HBM per device.

v0:
```python
import jax
import jax.numpy as jnp
from jax import lax
from jax.sharding import PartitionSpec as P

HEAD = 64
EPSILON = 1e-06


def layer_norm(rows, gain, shift):
    centre = rows - jnp.mean(rows, axis=-1, keepdims=True)
    spread = jnp.mean(centre * centre, axis=-1, keepdims=True)
    return centre * lax.rsqrt(spread + EPSILON) * gain + shift


def gelu_exact(values):
    return jax.nn.gelu(values, approximate=False)


def split_heads(values):
    return values.reshape(values.shape[:-1] + (values.shape[-1] // HEAD, HEAD))


def einsum_forms(temporal):
    if temporal:
        return ("qbhe,kbhe->bhqk", "bhqk,kbhe->qbhe", "bhqk,qbhe->kbhe")
    return ("bqhe,bkhe->bhqk", "bhqk,bkhe->bqhe", "bhqk,bqhe->bkhe")


def scores_of(queries, key_rows, temporal):
    score_form = einsum_forms(temporal)[0]
    return jnp.einsum(score_form, queries, key_rows, preferred_element_type=jnp.float32) * 0.125


def attend(triple, temporal):
    mix_form = einsum_forms(temporal)[1]
    queries, key_rows, value_rows = (
        split_heads(triple[0]),
        split_heads(triple[1]),
        split_heads(triple[2]),
    )
    scores = scores_of(queries, key_rows, temporal)
    highest = jnp.max(scores, axis=-1, keepdims=True)
    log_total = highest + jnp.log(jnp.sum(jnp.exp(scores - highest), axis=-1, keepdims=True))
    weights = jnp.exp(scores - log_total).astype(jnp.bfloat16)
    mixed = jnp.einsum(mix_form, weights, value_rows, preferred_element_type=jnp.float32)
    return (mixed.reshape(triple.shape[1:]).astype(jnp.bfloat16), log_total)


def attend_back(triple, log_total, grad_mixed, temporal):
    score_form, mix_form, back_form = einsum_forms(temporal)
    queries, key_rows, value_rows = (
        split_heads(triple[0]),
        split_heads(triple[1]),
        split_heads(triple[2]),
    )
    probs = jnp.exp(scores_of(queries, key_rows, temporal) - log_total)
    weights = probs.astype(jnp.bfloat16)
    grad_heads = split_heads(grad_mixed)
    grad_probs = jnp.einsum(score_form, grad_heads, value_rows, preferred_element_type=jnp.float32)
    inner = jnp.sum(probs * grad_probs, axis=-1, keepdims=True)
    grad_scores = (probs * (grad_probs - inner)).astype(jnp.bfloat16)
    grad_query = (
        jnp.einsum(mix_form, grad_scores, key_rows, preferred_element_type=jnp.float32) * 0.125
    )
    grad_key = (
        jnp.einsum(back_form, grad_scores, queries, preferred_element_type=jnp.float32) * 0.125
    )
    grad_value = jnp.einsum(back_form, weights, grad_heads, preferred_element_type=jnp.float32)
    stacked = jnp.stack([grad_query, grad_key, grad_value]).astype(jnp.bfloat16)
    return stacked.reshape(triple.shape)


def local(
    inputs,
    cotangent,
    norm_gain,
    norm_bias,
    attn_weight,
    attn_bias,
    out_weight,
    out_bias,
    up_weight,
    up_bias,
    down_weight,
    down_bias,
):
    width = attn_weight.shape[3]
    hidden_width = up_weight.shape[1]
    model_width = inputs.shape[3]
    tp_rank = lax.axis_index("tp")
    up_wide, down_wide = (up_weight, down_weight)
    up_bias_used = lax.dynamic_slice_in_dim(up_bias, tp_rank * hidden_width, hidden_width, 0)
    used_hidden = up_wide.shape[1]

    def fetch_weights():
        return (
            lax.all_gather(attn_weight, "fsdp", axis=2, tiled=True),
            lax.all_gather(out_weight, "fsdp", axis=2, tiled=True),
            lax.all_gather(up_wide, "fsdp", axis=0, tiled=True),
            lax.all_gather(down_wide, "fsdp", axis=1, tiled=True),
        )

    def spread_rows(values):
        return lax.all_gather(values, "tp", axis=1, tiled=True)

    def sum_rows(values):
        return lax.psum_scatter(
            values.astype(jnp.bfloat16), "tp", scatter_dimension=1, tiled=True
        ).astype(jnp.float32)

    def spread_grads(values):
        return lax.all_gather(values, "tp", axis=1, tiled=True)

    def sum_grads(values):
        return lax.psum_scatter(
            values.astype(jnp.bfloat16), "tp", scatter_dimension=1, tiled=True
        ).astype(jnp.float32)

    def attn_forward(stream, index, weights_all, temporal):
        attn_full, out_full = (weights_all[0], weights_all[1])
        normed = spread_rows(
            layer_norm(stream, norm_gain[index], norm_bias[index]).astype(jnp.bfloat16)
        )
        zero_row = jnp.zeros((width,), jnp.float32)
        bias_rows = jnp.stack([attn_bias[index, 0], zero_row, attn_bias[index, 1]])
        triple = jnp.einsum(
            "fpd,jdc->jfpc", normed, attn_full[index], preferred_element_type=jnp.float32
        )
        triple = (triple + bias_rows[:, None, None, :]).astype(jnp.bfloat16)
        if temporal:
            triple = lax.all_to_all(triple, "ctx", split_axis=2, concat_axis=1, tiled=True)
        mixed, log_total = attend(triple, temporal)
        if temporal:
            mixed = lax.all_to_all(mixed, "ctx", split_axis=0, concat_axis=1, tiled=True)
        partial_out = jnp.einsum(
            "fpc,cd->fpd", mixed, out_full[index], preferred_element_type=jnp.float32
        )
        stream_next = stream + (sum_rows(partial_out) + out_bias[index])
        return (stream_next, (normed, triple, log_total, mixed))

    def attn_backward(stream, index, weights_all, kept, grad_stream, temporal):
        attn_full, out_full = (weights_all[0], weights_all[1])
        normed, triple, log_total, mixed = kept
        grad_branch = grad_stream.astype(jnp.bfloat16)
        grad_bias_out = jnp.sum(grad_branch.astype(jnp.float32), axis=(0, 1))
        grad_full = spread_grads(grad_branch)
        grad_weight_out = jnp.einsum(
            "fpc,fpd->cd", mixed, grad_full, preferred_element_type=jnp.float32
        )
        grad_mixed = jnp.einsum(
            "fpd,cd->fpc", grad_full, out_full[index], preferred_element_type=jnp.float32
        ).astype(jnp.bfloat16)
        if temporal:
            grad_mixed = lax.all_to_all(grad_mixed, "ctx", split_axis=1, concat_axis=0, tiled=True)
        grad_triple = attend_back(triple, log_total, grad_mixed, temporal)
        if temporal:
            grad_triple = lax.all_to_all(
                grad_triple, "ctx", split_axis=1, concat_axis=2, tiled=True
            )
        grad_weight_attn = jnp.einsum(
            "fpd,jfpc->jdc", normed, grad_triple, preferred_element_type=jnp.float32
        )
        column_sums = jnp.sum(grad_triple.astype(jnp.float32), axis=(1, 2))
        grad_bias_attn = jnp.stack([column_sums[0], column_sums[2]])
        grad_normed = sum_grads(
            jnp.einsum(
                "jfpc,jdc->fpd", grad_triple, attn_full[index], preferred_element_type=jnp.float32
            )
        )
        unused, pull = jax.vjp(layer_norm, stream, norm_gain[index], norm_bias[index])
        grad_input, grad_gain, grad_shift = pull(grad_normed)
        return (
            grad_stream + grad_input,
            (
                grad_gain,
                grad_shift,
                grad_weight_attn,
                grad_bias_attn,
                grad_weight_out,
                grad_bias_out,
            ),
        )

    def mlp_forward(stream, weights_all):
        up_full, down_full = (weights_all[2], weights_all[3])
        normed = layer_norm(stream, norm_gain[2], norm_bias[2]).astype(jnp.bfloat16)
        normed = spread_rows(normed)
        hidden = (
            jnp.einsum("fpd,dc->fpc", normed, up_full, preferred_element_type=jnp.float32)
            + up_bias_used
        )
        active = gelu_exact(hidden).astype(jnp.bfloat16)
        partial_out = jnp.einsum(
            "fpc,cd->fpd", active, down_full, preferred_element_type=jnp.float32
        )
        partial_out = sum_rows(partial_out)
        return (stream + (partial_out + down_bias), (normed, hidden, active))

    def mlp_backward(stream, weights_all, kept, grad_stream):
        up_full, down_full = (weights_all[2], weights_all[3])
        normed, hidden, active = kept
        grad_branch = grad_stream.astype(jnp.bfloat16)
        grad_bias_down = jnp.sum(grad_branch.astype(jnp.float32), axis=(0, 1))
        grad_full = spread_grads(grad_branch)
        grad_weight_down = jnp.einsum(
            "fpc,fpd->cd", active, grad_full, preferred_element_type=jnp.float32
        )
        grad_active = jnp.einsum(
            "fpd,cd->fpc", grad_full, down_full, preferred_element_type=jnp.float32
        )
        unused, pull_gelu = jax.vjp(gelu_exact, hidden)
        grad_hidden = pull_gelu(grad_active)[0].astype(jnp.bfloat16)
        grad_bias_up = jnp.sum(grad_hidden.astype(jnp.float32), axis=(0, 1))
        grad_weight_up = jnp.einsum(
            "fpd,fpc->dc", normed, grad_hidden, preferred_element_type=jnp.float32
        )
        grad_normed = jnp.einsum(
            "fpc,dc->fpd", grad_hidden, up_full, preferred_element_type=jnp.float32
        )
        grad_normed = sum_grads(grad_normed)
        unused_ln, pull = jax.vjp(layer_norm, stream, norm_gain[2], norm_bias[2])
        grad_input, grad_gain, grad_shift = pull(grad_normed)
        return (
            grad_stream + grad_input,
            (grad_gain, grad_shift, grad_weight_up, grad_bias_up, grad_weight_down, grad_bias_down),
        )

    def step(totals, pair):
        clip, grad_clip = pair
        forward_weights = fetch_weights()
        backward_weights = fetch_weights()
        stream_first = clip.astype(jnp.float32)
        stream_second, kept_spatial = attn_forward(stream_first, 0, forward_weights, False)
        stream_third, kept_temporal = attn_forward(stream_second, 1, forward_weights, True)
        result, kept_mlp = mlp_forward(stream_third, forward_weights)
        grad_third, mlp_terms = mlp_backward(
            stream_third, backward_weights, kept_mlp, grad_clip.astype(jnp.float32)
        )
        grad_second, temporal_terms = attn_backward(
            stream_second, 1, backward_weights, kept_temporal, grad_third, True
        )
        grad_first, spatial_terms = attn_backward(
            stream_first, 0, backward_weights, kept_spatial, grad_second, False
        )
        increments = (
            jnp.stack([spatial_terms[0], temporal_terms[0], mlp_terms[0]]),
            jnp.stack([spatial_terms[1], temporal_terms[1], mlp_terms[1]]),
            jnp.stack([spatial_terms[2], temporal_terms[2]]),
            jnp.stack([spatial_terms[3], temporal_terms[3]]),
            jnp.stack([spatial_terms[4], temporal_terms[4]]),
            jnp.stack([spatial_terms[5], temporal_terms[5]]),
            mlp_terms[2],
            mlp_terms[3],
            mlp_terms[4],
            mlp_terms[5],
        )
        totals = jax.tree.map(jnp.add, totals, increments)
        return (totals, (result.astype(jnp.bfloat16), grad_first.astype(jnp.bfloat16)))

    start = (
        jnp.zeros((3, model_width), jnp.float32),
        jnp.zeros((3, model_width), jnp.float32),
        jnp.zeros((2, 3, model_width, width), jnp.float32),
        jnp.zeros((2, 2, width), jnp.float32),
        jnp.zeros((2, width, model_width), jnp.float32),
        jnp.zeros((2, model_width), jnp.float32),
        jnp.zeros((model_width, used_hidden), jnp.float32),
        jnp.zeros((used_hidden,), jnp.float32),
        jnp.zeros((used_hidden, model_width), jnp.float32),
        jnp.zeros((model_width,), jnp.float32),
    )
    totals, stacked = lax.scan(step, start, (inputs, cotangent))
    up_total, down_total = (totals[6], totals[8])
    up_bias_full = lax.dynamic_update_slice_in_dim(
        jnp.zeros((hidden_width * lax.axis_size("tp"),), jnp.float32),
        totals[7],
        tp_rank * hidden_width,
        0,
    )
    matrices = (
        lax.psum_scatter(totals[2], ("fsdp", "ctx"), scatter_dimension=2, tiled=True),
        lax.psum_scatter(totals[4], ("fsdp", "ctx"), scatter_dimension=2, tiled=True),
        lax.psum_scatter(up_total, ("fsdp", "ctx"), scatter_dimension=0, tiled=True),
        lax.psum_scatter(down_total, ("fsdp", "ctx"), scatter_dimension=1, tiled=True),
    )
    attn_bias_full = lax.dynamic_update_slice_in_dim(
        jnp.zeros((2, 2, model_width), jnp.float32), totals[3], tp_rank * width, 2
    )
    vectors = lax.psum(
        (totals[0], totals[1], attn_bias_full, totals[5], up_bias_full, totals[9]),
        ("fsdp", "ctx", "tp"),
    )
    attn_bias_part = lax.dynamic_slice_in_dim(vectors[2], tp_rank * width, width, 2)
    return (
        stacked[0],
        stacked[1],
        vectors[0],
        vectors[1],
        matrices[0],
        attn_bias_part,
        matrices[1],
        vectors[3],
        matrices[2],
        vectors[4],
        matrices[3],
        vectors[5],
    )


def solution(mesh):
    return jax.shard_map(
        local,
        mesh=mesh,
        in_specs=(
            P("fsdp", "ctx", "tp", None),
            P("fsdp", "ctx", "tp", None),
            P(),
            P(),
            P(None, None, "fsdp", "tp"),
            P(None, None, "tp"),
            P(None, "tp", "fsdp"),
            P(),
            P("fsdp", "tp"),
            P(),
            P("tp", "fsdp"),
            P(),
        ),
        out_specs=(
            P("fsdp", "ctx", "tp", None),
            P("fsdp", "ctx", "tp", None),
            P(),
            P(),
            P(None, None, ("fsdp", "ctx"), "tp"),
            P(None, None, "tp"),
            P(None, "tp", ("fsdp", "ctx")),
            P(),
            P(("fsdp", "ctx"), "tp"),
            P(),
            P("tp", ("fsdp", "ctx")),
            P(),
        ),
        check_vma=False,
    )
```

profile of v0, /device:TPU:0, one launch (start us, length us, event | category | flops | bytes accessed | tf_op | source)
XLA Modules:
  0.0 1763.9 jit_solution(5922801304353576764)
XLA Ops:
  9.5 1556.3 %while.33 = (s32[]{:T(128)}, f32[3,768]{1,0:T(4,128)}, f32[3,768]{1,0:T(4,128)}, f32[2,3,768,192]{2,3,1,0:T(8,128)}, f32[2,2,192]{2,1,0:T(2,128)}, /*index=5*/f3...) while((s32[]{:T(128)}, f32[3,768]{1,0:T(4,128)}, ...), condition=%wide.region_37.0_spmd.clone, body=%wide.region_0.37_spmd.clone.sunk | while | flops 11599428608 | bytes 431165984 | solution.py:273
  16.3 14.6 all_gather.55
  30.9 15.2 all-gather.18.cloned.1.call-done
  46.1 34.4 %all-gather.16.cloned.1.call-done = bf16[4,196,768]{2,0,1:T(4,128)(2,1)} async-done(((bf16[4,49,768]{2,0,1:T(4,128)(2,1)}), bf16[4,196,768]{2,0,1:T(4,128)(2,1)}) %all-gather.16.cloned.1.call-update) | async-done | bytes 1204240 | tf_op jit(solution)/shard_map/while/body/eval_jaxpr/all_gather | solution.py:105
  89.9 54.9 %all-reduce.24.cloned.1.call-done = bf16[4,196,768]{2,0,1:T(4,128)(2,1)} async-done(((bf16[4,196,768]{2,0,1:T(4,128)(2,1)}), bf16[4,196,768]{2,0,1:T(4,128)(2,1)}) %all-reduce.24.cloned.1.call-update) | async-done | bytes 1204240 | tf_op jit(solution)/shard_map/while
  149.7 30.2 %all-gather.20.cloned.1.call-done = bf16[4,196,768]{2,0,1:T(4,128)(2,1)} async-done(((bf16[4,49,768]{2,0,1:T(4,128)(2,1)}), bf16[4,196,768]{2,0,1:T(4,128)(2,1)}) %all-gather.20.cloned.1.call-update) | async-done | bytes 1204240 | tf_op jit(solution)/shard_map/while/body/eval_jaxpr/all_gather | solution.py:105
  187.1 20.1 %all_to_all.74 = bf16[3,4,196,192]{3,1,0,2:T(4,128)(2,1)S(1)} all-to-all(bf16[3,4,196,192]{3,1,0,2:T(4,128)(2,1)} %copy.354), channel_id=1, replica_groups=mesh['fsdp'=2,'ctx'=4,'tp'=4] {'ctx'}, dimensions={2} | all-to-all | bytes 1806336 | tf_op jit(solution)/shard_map/while/body/eval_jaxpr/all_to_all | solution.py:132
  227.6 11.7 all_to_all.75
  245.9 54.7 %all-reduce.26.cloned.1.call-done = bf16[4,196,768]{2,0,1:T(4,128)(2,1)} async-done(((bf16[4,196,768]{2,0,1:T(4,128)(2,1)}), bf16[4,196,768]{2,0,1:T(4,128)(2,1)}) %all-reduce.26.cloned.1.call-update) | async-done | bytes 1204240 | tf_op jit(solution)/shard_map/while
  306.5 17.8 %all-gather.14.cloned.1.call-done = bf16[768,768]{1,0:T(8,128)(2,1)} async-done(((bf16[384,768]{1,0:T(8,128)(2,1)}), bf16[768,768]{1,0:T(8,128)(2,1)}) %all-gather.14.cloned.1.call-update) | async-done | bytes 1179664 | tf_op jit(solution)/shard_map/while/body/eval_jaxpr/all_gather | solution.py:100
  324.3 32.9 %all-gather.22.cloned.1.call-done = bf16[4,196,768]{2,0,1:T(4,128)(2,1)} async-done(((bf16[4,49,768]{2,0,1:T(4,128)(2,1)}), bf16[4,196,768]{2,0,1:T(4,128)(2,1)}) %all-gather.22.cloned.1.call-update) | async-done | bytes 1204240 | tf_op jit(solution)/shard_map/while/body/eval_jaxpr/all_gather | solution.py:105
  361.9 6.8 multiply_convert_fusion.6
  368.7 12.0 all-gather.24.cloned.1.call-done
  380.7 32.3 %all-gather.26.cloned.1.call-done = bf16[1,4,196,768]{3,1,0,2:T(4,128)(2,1)} async-done(((bf16[1,4,49,768]{3,1,0,2:T(4,128)(2,1)}), bf16[1,4,196,768]{3,1,0,2:T(4,128)(2,1)}) %all-gather.26.cloned.1.call-update) | async-done | bytes 1204240 | tf_op jit(solution)/shard_map/while/body/eval_jaxpr/all_gather | solution.py:113
  413.0 5.7 convert_reduce_fusion.20
  421.4 56.2 %all-reduce.28.cloned.1.call-done = bf16[4,196,768]{2,0,1:T(4,128)(2,1)} async-done(((bf16[4,196,768]{2,0,1:T(4,128)(2,1)}), bf16[4,196,768]{2,0,1:T(4,128)(2,1)}) %all-reduce.28.cloned.1.call-update) | async-done | bytes 1204240 | tf_op jit(solution)/shard_map/while
  485.1 30.2 %all-gather.28.cloned.1.call-done = bf16[4,196,768]{2,0,1:T(4,128)(2,1)} async-done(((bf16[4,49,768]{2,0,1:T(4,128)(2,1)}), bf16[4,196,768]{2,0,1:T(4,128)(2,1)}) %all-gather.28.cloned.1.call-update) | async-done | bytes 1204240 | tf_op jit(solution)/shard_map/while/body/eval_jaxpr/all_gather | solution.py:113
  520.0 11.1 all_to_all.76
  555.3 20.4 %all_to_all.77 = bf16[3,16,49,192]{3,2,0,1:T(8,128)(2,1)S(1)} all-to-all(bf16[3,16,49,192]{3,2,0,1:T(8,128)(2,1)S(1)} %copy.369), channel_id=1, replica_groups=mesh['fsdp'=2,'ctx'=4,'tp'=4] {'ctx'}, dimensions={1} | all-to-all | bytes 1806336 | tf_op jit(solution)/shard_map/while/body/eval_jaxpr/all_to_all | solution.py:158
  586.4 49.8 %all-reduce.30.cloned.1.call-done = bf16[4,196,768]{2,0,1:T(4,128)(2,1)} async-done(((bf16[4,196,768]{2,0,1:T(4,128)(2,1)}), bf16[4,196,768]{2,0,1:T(4,128)(2,1)}) %all-reduce.30.cloned.1.call-update) | async-done | bytes 1204240 | tf_op jit(solution)/shard_map/while
  657.8 17.7 %all-gather.30.cloned.1.call-done = bf16[4,196,768]{2,0,1:T(4,128)(2,1)} async-done(((bf16[4,49,768]{2,0,1:T(4,128)(2,1)}), bf16[4,196,768]{2,0,1:T(4,128)(2,1)}) %all-gather.30.cloned.1.call-update) | async-done | bytes 1204240 | tf_op jit(solution)/shard_map/while/body/eval_jaxpr/all_gather | solution.py:113
  694.8 86.4 %all-reduce.32.cloned.1.call-done = (bf16[4,196,768]{2,0,1:T(4,128)(2,1)}, bf16[4,196,768]{2,0,1:T(4,128)(2,1)}) async-done(((bf16[4,196,768]{2,0,1:T(4,128)(2,1)}, bf16[4,196,768]{2,0,1:T(4,128)(2,1)}), (bf16[4,196,768]{2,0,1:T(4,128)(2,1)}, bf16[4,196,768]{2,0,1:T(4,128)(2,1)})) %all-reduce.32.cloned.1.call-update) | async-done | bytes 2408464 | tf_op jit(solution)/shard_map/while
  794.5 15.3 all_gather.55
  809.9 13.1 all-gather.18.cloned.1.call-done
  822.9 31.8 %all-gather.16.cloned.1.call-done = bf16[4,196,768]{2,0,1:T(4,128)(2,1)} async-done(((bf16[4,49,768]{2,0,1:T(4,128)(2,1)}), bf16[4,196,768]{2,0,1:T(4,128)(2,1)}) %all-gather.16.cloned.1.call-update) | async-done | bytes 1204240 | tf_op jit(solution)/shard_map/while/body/eval_jaxpr/all_gather | solution.py:105
  864.2 54.9 %all-reduce.24.cloned.1.call-done = bf16[4,196,768]{2,0,1:T(4,128)(2,1)} async-done(((bf16[4,196,768]{2,0,1:T(4,128)(2,1)}), bf16[4,196,768]{2,0,1:T(4,128)(2,1)}) %all-reduce.24.cloned.1.call-update) | async-done | bytes 1204240 | tf_op jit(solution)/shard_map/while
  924.0 30.2 %all-gather.20.cloned.1.call-done = bf16[4,196,768]{2,0,1:T(4,128)(2,1)} async-done(((bf16[4,49,768]{2,0,1:T(4,128)(2,1)}), bf16[4,196,768]{2,0,1:T(4,128)(2,1)}) %all-gather.20.cloned.1.call-update) | async-done | bytes 1204240 | tf_op jit(solution)/shard_map/while/body/eval_jaxpr/all_gather | solution.py:105
  961.3 19.8 %all_to_all.74 = bf16[3,4,196,192]{3,1,0,2:T(4,128)(2,1)S(1)} all-to-all(bf16[3,4,196,192]{3,1,0,2:T(4,128)(2,1)} %copy.354), channel_id=1, replica_groups=mesh['fsdp'=2,'ctx'=4,'tp'=4] {'ctx'}, dimensions={2} | all-to-all | bytes 1806336 | tf_op jit(solution)/shard_map/while/body/eval_jaxpr/all_to_all | solution.py:132
  1001.7 11.7 all_to_all.75
  1020.0 54.7 %all-reduce.26.cloned.1.call-done = bf16[4,196,768]{2,0,1:T(4,128)(2,1)} async-done(((bf16[4,196,768]{2,0,1:T(4,128)(2,1)}), bf16[4,196,768]{2,0,1:T(4,128)(2,1)}) %all-reduce.26.cloned.1.call-update) | async-done | bytes 1204240 | tf_op jit(solution)/shard_map/while
  1080.8 17.5 all-gather.14.cloned.1.call-done
  1098.4 32.9 %all-gather.22.cloned.1.call-done = bf16[4,196,768]{2,0,1:T(4,128)(2,1)} async-done(((bf16[4,49,768]{2,0,1:T(4,128)(2,1)}), bf16[4,196,768]{2,0,1:T(4,128)(2,1)}) %all-gather.22.cloned.1.call-update) | async-done | bytes 1204240 | tf_op jit(solution)/shard_map/while/body/eval_jaxpr/all_gather | solution.py:105
  1136.0 6.8 multiply_convert_fusion.6
  1142.7 12.0 all-gather.24.cloned.1.call-done
  1154.8 32.3 %all-gather.26.cloned.1.call-done = bf16[1,4,196,768]{3,1,0,2:T(4,128)(2,1)} async-done(((bf16[1,4,49,768]{3,1,0,2:T(4,128)(2,1)}), bf16[1,4,196,768]{3,1,0,2:T(4,128)(2,1)}) %all-gather.26.cloned.1.call-update) | async-done | bytes 1204240 | tf_op jit(solution)/shard_map/while/body/eval_jaxpr/all_gather | solution.py:113
  1187.1 5.7 convert_reduce_fusion.20
  1195.5 56.2 %all-reduce.28.cloned.1.call-done = bf16[4,196,768]{2,0,1:T(4,128)(2,1)} async-done(((bf16[4,196,768]{2,0,1:T(4,128)(2,1)}), bf16[4,196,768]{2,0,1:T(4,128)(2,1)}) %all-reduce.28.cloned.1.call-update) | async-done | bytes 1204240 | tf_op jit(solution)/shard_map/while
  1259.1 30.2 %all-gather.28.cloned.1.call-done = bf16[4,196,768]{2,0,1:T(4,128)(2,1)} async-done(((bf16[4,49,768]{2,0,1:T(4,128)(2,1)}), bf16[4,196,768]{2,0,1:T(4,128)(2,1)}) %all-gather.28.cloned.1.call-update) | async-done | bytes 1204240 | tf_op jit(solution)/shard_map/while/body/eval_jaxpr/all_gather | solution.py:113
  1294.1 11.1 all_to_all.76
  1329.3 20.4 %all_to_all.77 = bf16[3,16,49,192]{3,2,0,1:T(8,128)(2,1)S(1)} all-to-all(bf16[3,16,49,192]{3,2,0,1:T(8,128)(2,1)S(1)} %copy.369), channel_id=1, replica_groups=mesh['fsdp'=2,'ctx'=4,'tp'=4] {'ctx'}, dimensions={1} | all-to-all | bytes 1806336 | tf_op jit(solution)/shard_map/while/body/eval_jaxpr/all_to_all | solution.py:158
  1360.4 49.8 %all-reduce.30.cloned.1.call-done = bf16[4,196,768]{2,0,1:T(4,128)(2,1)} async-done(((bf16[4,196,768]{2,0,1:T(4,128)(2,1)}), bf16[4,196,768]{2,0,1:T(4,128)(2,1)}) %all-reduce.30.cloned.1.call-update) | async-done | bytes 1204240 | tf_op jit(solution)/shard_map/while
  1431.6 17.9 %all-gather.30.cloned.1.call-done = bf16[4,196,768]{2,0,1:T(4,128)(2,1)} async-done(((bf16[4,49,768]{2,0,1:T(4,128)(2,1)}), bf16[4,196,768]{2,0,1:T(4,128)(2,1)}) %all-gather.30.cloned.1.call-update) | async-done | bytes 1204240 | tf_op jit(solution)/shard_map/while/body/eval_jaxpr/all_gather | solution.py:113
  1470.9 84.3 %all-reduce.32.cloned.1.call-done = (bf16[4,196,768]{2,0,1:T(4,128)(2,1)}, bf16[4,196,768]{2,0,1:T(4,128)(2,1)}) async-done(((bf16[4,196,768]{2,0,1:T(4,128)(2,1)}, bf16[4,196,768]{2,0,1:T(4,128)(2,1)}), (bf16[4,196,768]{2,0,1:T(4,128)(2,1)}, bf16[4,196,768]{2,0,1:T(4,128)(2,1)})) %all-reduce.32.cloned.1.call-update) | async-done | bytes 2408464 | tf_op jit(solution)/shard_map/while
  1574.5 5.7 copy.195
  1581.2 40.8 %all-reduce.7 = (f32[3,768]{1,0:T(4,128)}, f32[3,768]{1,0:T(4,128)}, f32[2,2,768]{2,1,0:T(2,128)S(1)}, f32[2,768]{1,0:T(2,128)}, f32[3072]{0:T(1024)}, /*index=5*/f32[768]{0:T(1024)}) all-reduce(f32[3,768]{1,0:T(4,128)S(1)} %copy-done.64, f32[3,768]{1,0:T(4,128)S(1)} %copy-done.67, ...), channel_id=1, replica_groups=mesh['fsdp'=2,'ctx'=4,'tp'=4] {'fsdp','ctx','tp'}, use_global_device_ids=true, to_apply=%region_38.0 | all-reduce | flops 13056 | bytes 104448 | tf_op jit(solution)/shard_map/psum | solution.py:290
  1624.6 27.9 %reduce-scatter.11.cloned.1.call-done = f32[768,96]{0,1:T(8,128)} async-done(((f32[768,768]{0,1:T(8,128)}), f32[768,96]{0,1:T(8,128)}) %reduce-scatter.11.cloned.1.call-update) | async-done | bytes 294928 | tf_op jit(solution)/shard_map/reduce_scatter | solution.py:285
  1652.5 46.1 %reduce-scatter.9.cloned.1.call-done = f32[96,768]{1,0:T(8,128)} async-done(((f32[768,768]{1,0:T(8,128)}), f32[96,768]{1,0:T(8,128)}) %reduce-scatter.9.cloned.1.call-update) | async-done | bytes 294928 | tf_op jit(solution)/shard_map/reduce_scatter | solution.py:284
  1698.6 57.6 %reduce-scatter.7.cloned.1.call-done = f32[2,3,96,192]{3,2,1,0:T(8,128)} async-done(((f32[2,3,768,192]{3,2,1,0:T(8,128)}), f32[2,3,96,192]{3,2,1,0:T(8,128)}) %reduce-scatter.7.cloned.1.call-update) | async-done | bytes 442384 | tf_op jit(solution)/shard_map/reduce_scatter | solution.py:282
  (734 shorter events, 337.6 us)
Async XLA Ops:
  9.5 36.6 %all-gather.18.cloned.1.call-start = ((), (), s32[]{:S(2)}) async-start(), calls=%async_computation.14 | async-start | bytes 2654208 | tf_op jit(solution)/shard_map/while/body/eval_jaxpr/all_gather | solution.py:98
  10.2 70.2 %all-gather.16.cloned.1.call-start = ((), (), s32[]{:S(2)}) async-start(), calls=%async_computation.13 | async-start | bytes 1505280 | tf_op jit(solution)/shard_map/while/body/eval_jaxpr/all_gather | solution.py:105
  12.3 135.2 %copy-start.54 = (f32[768]{0:T(1024)}, f32[768]{0:T(1024)S(1)}, u32[]{:S(2)}) copy-start(f32[768]{0:T(1024)S(1)} %get-tuple-element.649) | copy-start | bytes 9220 | tf_op jit(solution)/shard_map/while
  16.2 128.7 %all-reduce.24.cloned.1.call-start = ((), (), s32[]{:S(2)}) async-start(), calls=%async_computation.15 | async-start | bytes 2408448 | tf_op jit(solution)/shard_map/while
  88.6 91.4 %all-gather.20.cloned.1.call-start = ((), (), s32[]{:S(2)}) async-start(), calls=%async_computation.16 | async-start | bytes 1505280 | tf_op jit(solution)/shard_map/while/body/eval_jaxpr/all_gather | solution.py:105
  149.6 151.0 %all-reduce.26.cloned.1.call-start = ((), (), s32[]{:S(2)}) async-start(), calls=%async_computation.17 | async-start | bytes 2408448 | tf_op jit(solution)/shard_map/while
  245.3 79.0 %all-gather.14.cloned.1.call-start = ((), (), s32[]{:S(2)}) async-start(), calls=%async_computation.12 | async-start | bytes 1769472 | tf_op jit(solution)/shard_map/while/body/eval_jaxpr/all_gather | solution.py:100
  245.9 111.3 %all-gather.22.cloned.1.call-start = ((), (), s32[]{:S(2)}) async-start(), calls=%async_computation.18 | async-start | bytes 1505280 | tf_op jit(solution)/shard_map/while/body/eval_jaxpr/all_gather | solution.py:105
  302.6 179.5 %copy-start.36 = (f32[4,49]{0,1:T(8,128)}, f32[4,49]{0,1:T(8,128)S(1)}, u32[]{:S(2)}) copy-start(f32[4,49]{0,1:T(8,128)S(1)} %fusion.242) | copy-start | bytes 2356 | tf_op jit(solution)/shard_map/while
  303.6 77.1 %all-gather.24.cloned.1.call-start = ((), (), s32[]{:S(2)}) async-start(), calls=%async_computation.19 | async-start | bytes 1769472 | tf_op jit(solution)/shard_map/while/body/eval_jaxpr/all_gather | solution.py:101
  304.4 108.6 %all-gather.26.cloned.1.call-start = ((), (), s32[]{:S(2)}) async-start(), calls=%async_computation.20 | async-start | bytes 1505280 | tf_op jit(solution)/shard_map/while/body/eval_jaxpr/all_gather | solution.py:113
  306.3 171.4 %all-reduce.28.cloned.1.call-start = ((), (), s32[]{:S(2)}) async-start(), calls=%async_computation.21 | async-start | bytes 2408448 | tf_op jit(solution)/shard_map/while
  421.3 94.0 %all-gather.28.cloned.1.call-start = ((), (), s32[]{:S(2)}) async-start(), calls=%async_computation.22 | async-start | bytes 1505280 | tf_op jit(solution)/shard_map/while/body/eval_jaxpr/all_gather | solution.py:113
  485.0 151.1 %all-reduce.30.cloned.1.call-start = ((), (), s32[]{:S(2)}) async-start(), calls=%async_computation.23 | async-start | bytes 2408448 | tf_op jit(solution)/shard_map/while
  580.8 94.7 %all-gather.30.cloned.1.call-start = ((), (), s32[]{:S(2)}) async-start(), calls=%async_computation.24 | async-start | bytes 1505280 | tf_op jit(solution)/shard_map/while/body/eval_jaxpr/all_gather | solution.py:113
  645.2 136.0 %all-reduce.32.cloned.1.call-start = ((), (), s32[]{:S(2)}) async-start(), calls=%async_computation.25 | async-start | bytes 4816896 | tf_op jit(solution)/shard_map/while
  692.5 88.7 %copy-start.4 = (bf16[2,4,49,768]{3,1,2,0:T(4,128)(2,1)S(1)}, bf16[2,4,49,768]{3,1,2,0:T(4,128)(2,1)}, u32[]{:S(2)}) copy-start(bf16[2,4,49,768]{3,1,2,0:T(4,128)(2,1)} %get-tuple-element.787) | copy-start | bytes 1806340 | tf_op jit(solution)/shard_map/while
  692.5 88.7 %copy-start.57 = (f32[768]{0:T(1024)S(1)}, f32[768]{0:T(1024)}, u32[]{:S(2)}) copy-start(f32[768]{0:T(1024)} %copy-done.56) | copy-start | bytes 9220 | tf_op jit(solution)/shard_map/while
  692.5 90.1 %copy-start.51 = (f32[4,49]{0,1:T(8,128)S(1)}, f32[4,49]{0,1:T(8,128)}, u32[]{:S(2)}) copy-start(f32[4,49]{0,1:T(8,128)} %copy-done.50) | copy-start | bytes 2356 | tf_op jit(solution)/shard_map/while
  692.5 90.1 %copy-start.40 = (f32[4,49]{0,1:T(8,128)S(1)}, f32[4,49]{0,1:T(8,128)}, u32[]{:S(2)}) copy-start(f32[4,49]{0,1:T(8,128)} %copy-done.39) | copy-start | bytes 2356 | tf_op jit(solution)/shard_map/while
  692.5 91.9 %copy-start.89 = (f32[768]{0:T(1024)S(1)}, f32[768]{0:T(1024)}, u32[]{:S(2)}) copy-start(f32[768]{0:T(1024)} %get-tuple-element.798) | copy-start | bytes 9220 | tf_op jit(solution)/shard_map/while
  694.8 89.6 %copy-start.21 = (f32[4,49,768]{2,0,1:T(4,128)S(1)}, f32[4,49,768]{2,0,1:T(4,128)}, u32[]{:S(2)}) copy-start(f32[4,49,768]{2,0,1:T(4,128)} %get-tuple-element.706) | copy-start | bytes 1806340 | tf_op jit(solution)/shard_map/while
  787.8 35.1 %all-gather.18.cloned.1.call-start = ((), (), s32[]{:S(2)}) async-start(), calls=%async_computation.14 | async-start | bytes 2654208 | tf_op jit(solution)/shard_map/while/body/eval_jaxpr/all_gather | solution.py:98
  788.4 66.3 %all-gather.16.cloned.1.call-start = ((), (), s32[]{:S(2)}) async-start(), calls=%async_computation.13 | async-start | bytes 1505280 | tf_op jit(solution)/shard_map/while/body/eval_jaxpr/all_gather | solution.py:105
  790.5 131.3 %copy-start.54 = (f32[768]{0:T(1024)}, f32[768]{0:T(1024)S(1)}, u32[]{:S(2)}) copy-start(f32[768]{0:T(1024)S(1)} %get-tuple-element.649) | copy-start | bytes 9220 | tf_op jit(solution)/shard_map/while
  794.4 124.8 %all-reduce.24.cloned.1.call-start = ((), (), s32[]{:S(2)}) async-start(), calls=%async_computation.15 | async-start | bytes 2408448 | tf_op jit(solution)/shard_map/while
  862.9 91.3 %all-gather.20.cloned.1.call-start = ((), (), s32[]{:S(2)}) async-start(), calls=%async_computation.16 | async-start | bytes 1505280 | tf_op jit(solution)/shard_map/while/body/eval_jaxpr/all_gather | solution.py:105
  923.9 150.8 %all-reduce.26.cloned.1.call-start = ((), (), s32[]{:S(2)}) async-start(), calls=%async_computation.17 | async-start | bytes 2408448 | tf_op jit(solution)/shard_map/while
  1019.4 79.0 %all-gather.14.cloned.1.call-start = ((), (), s32[]{:S(2)}) async-start(), calls=%async_computation.12 | async-start | bytes 1769472 | tf_op jit(solution)/shard_map/while/body/eval_jaxpr/all_gather | solution.py:100
  1020.0 111.3 %all-gather.22.cloned.1.call-start = ((), (), s32[]{:S(2)}) async-start(), calls=%async_computation.18 | async-start | bytes 1505280 | tf_op jit(solution)/shard_map/while/body/eval_jaxpr/all_gather | solution.py:105
  1076.6 179.5 %copy-start.36 = (f32[4,49]{0,1:T(8,128)}, f32[4,49]{0,1:T(8,128)S(1)}, u32[]{:S(2)}) copy-start(f32[4,49]{0,1:T(8,128)S(1)} %fusion.242) | copy-start | bytes 2356 | tf_op jit(solution)/shard_map/while
  1077.7 77.1 %all-gather.24.cloned.1.call-start = ((), (), s32[]{:S(2)}) async-start(), calls=%async_computation.19 | async-start | bytes 1769472 | tf_op jit(solution)/shard_map/while/body/eval_jaxpr/all_gather | solution.py:101
  1078.4 108.6 %all-gather.26.cloned.1.call-start = ((), (), s32[]{:S(2)}) async-start(), calls=%async_computation.20 | async-start | bytes 1505280 | tf_op jit(solution)/shard_map/while/body/eval_jaxpr/all_gather | solution.py:113
  1080.3 171.4 %all-reduce.28.cloned.1.call-start = ((), (), s32[]{:S(2)}) async-start(), calls=%async_computation.21 | async-start | bytes 2408448 | tf_op jit(solution)/shard_map/while
  1195.4 94.0 %all-gather.28.cloned.1.call-start = ((), (), s32[]{:S(2)}) async-start(), calls=%async_computation.22 | async-start | bytes 1505280 | tf_op jit(solution)/shard_map/while/body/eval_jaxpr/all_gather | solution.py:113
  1259.1 151.1 %all-reduce.30.cloned.1.call-start = ((), (), s32[]{:S(2)}) async-start(), calls=%async_computation.23 | async-start | bytes 2408448 | tf_op jit(solution)/shard_map/while
  1354.8 94.7 %all-gather.30.cloned.1.call-start = ((), (), s32[]{:S(2)}) async-start(), calls=%async_computation.24 | async-start | bytes 1505280 | tf_op jit(solution)/shard_map/while/body/eval_jaxpr/all_gather | solution.py:113
  1419.2 136.0 %all-reduce.32.cloned.1.call-start = ((), (), s32[]{:S(2)}) async-start(), calls=%async_computation.25 | async-start | bytes 4816896 | tf_op jit(solution)/shard_map/while
  1466.5 88.7 %copy-start.4 = (bf16[2,4,49,768]{3,1,2,0:T(4,128)(2,1)S(1)}, bf16[2,4,49,768]{3,1,2,0:T(4,128)(2,1)}, u32[]{:S(2)}) copy-start(bf16[2,4,49,768]{3,1,2,0:T(4,128)(2,1)} %get-tuple-element.787) | copy-start | bytes 1806340 | tf_op jit(solution)/shard_map/while
  1466.5 88.7 %copy-start.57 = (f32[768]{0:T(1024)S(1)}, f32[768]{0:T(1024)}, u32[]{:S(2)}) copy-start(f32[768]{0:T(1024)} %copy-done.56) | copy-start | bytes 9220 | tf_op jit(solution)/shard_map/while
  1466.5 90.1 %copy-start.51 = (f32[4,49]{0,1:T(8,128)S(1)}, f32[4,49]{0,1:T(8,128)}, u32[]{:S(2)}) copy-start(f32[4,49]{0,1:T(8,128)} %copy-done.50) | copy-start | bytes 2356 | tf_op jit(solution)/shard_map/while
  1466.5 90.1 %copy-start.40 = (f32[4,49]{0,1:T(8,128)S(1)}, f32[4,49]{0,1:T(8,128)}, u32[]{:S(2)}) copy-start(f32[4,49]{0,1:T(8,128)} %copy-done.39) | copy-start | bytes 2356 | tf_op jit(solution)/shard_map/while
  1466.6 92.0 %copy-start.89 = (f32[768]{0:T(1024)S(1)}, f32[768]{0:T(1024)}, u32[]{:S(2)}) copy-start(f32[768]{0:T(1024)} %get-tuple-element.798) | copy-start | bytes 9220 | tf_op jit(solution)/shard_map/while
  1470.9 87.6 %copy-start.21 = (f32[4,49,768]{2,0,1:T(4,128)S(1)}, f32[4,49,768]{2,0,1:T(4,128)}, u32[]{:S(2)}) copy-start(f32[4,49,768]{2,0,1:T(4,128)} %get-tuple-element.706) | copy-start | bytes 1806340 | tf_op jit(solution)/shard_map/while
  1565.8 56.9 %reduce-scatter.13.cloned.1.call-start = ((), (), s32[]{:S(2)}) async-start(), calls=%async_computation.11 | async-start | bytes 1327104
  1570.6 81.9 %reduce-scatter.11.cloned.1.call-start = ((), (), s32[]{:S(2)}) async-start(), calls=%async_computation.10 | async-start | bytes 2654208 | tf_op jit(solution)/shard_map/reduce_scatter | solution.py:285
  1573.8 124.7 %reduce-scatter.9.cloned.1.call-start = ((), (), s32[]{:S(2)}) async-start(), calls=%async_computation.9 | async-start | bytes 2654208 | tf_op jit(solution)/shard_map/reduce_scatter | solution.py:284
  1574.4 181.7 %reduce-scatter.7.cloned.1.call-start = ((), (), s32[]{:S(2)}) async-start(), calls=%async_computation.8 | async-start | bytes 5308416 | tf_op jit(solution)/shard_map/reduce_scatter | solution.py:282
  (180 other events, 2109.2 us)
Sparse Core Ops, SparseCore 0:
  11.8 34.2 all-gather.17
  48.3 32.1 all-gather.15
  88.7 56.1 all-reduce.23
  149.7 30.1 all-gather.19
  245.4 55.1 all-reduce.25
  302.1 22.2 all-gather.13
  326.4 30.6 all-gather.21
  358.7 21.9 all-gather.23
  382.3 30.6 all-gather.25
  421.5 56.1 all-reduce.27
  485.1 30.1 all-gather.27
  580.9 55.1 all-reduce.29
  645.3 30.1 all-gather.29
  685.3 95.8 all-reduce.31
  789.9 33.0 all-gather.17
  824.9 29.7 all-gather.15
  863.0 56.0 all-reduce.23
  924.0 30.1 all-gather.19
  1019.5 55.1 all-reduce.25
  1076.1 22.2 all-gather.13
  1100.5 30.6 all-gather.21
  1132.8 21.9 all-gather.23
  1156.3 30.6 all-gather.25
  1195.5 56.1 all-reduce.27
  1259.2 30.1 all-gather.27
  1355.0 55.1 all-reduce.29
  1419.4 30.1 all-gather.29
  1459.3 95.8 all-reduce.31
Sparse Core Ops, SparseCore 1:
  1570.7 35.7 reduce-scatter.12
  1610.2 42.2 reduce-scatter.10
  1656.3 42.2 reduce-scatter.8
  1702.6 53.5 reduce-scatter.6
where the time goes:
time: 1770 us; the launch traced here: 1760 us
  waiting for transfers between devices  1180 us (67%)
  blocking collectives  197 us (11%)
  local copies, waits for them, and re-layouts  154 us (9%)
  matrix products  108 us (6%)
  other arithmetic  98.1 us (6%)
    while x38, waiting for transfers between devices  606 us
    all_gather x6, waiting for transfers between devices, spread_rows(): return lax.all_gather(values, 'tp', axis=1, tiled=True)  192 us
    all_gather x6, waiting for transfers between devices, spread_grads(): return lax.all_gather(values, 'tp', axis=1, tiled=True)  161 us
    reduce_scatter x1, waiting for transfers between devices, local(): lax.psum_scatter(totals[2], ('fsdp', 'ctx'), scatter_dimension=2, tiled=T...  57.6 us
    reduce_scatter x1, waiting for transfers between devices, local(): lax.psum_scatter(up_total, ('fsdp', 'ctx'), scatter_dimension=0, tiled=True)  46.1 us
    psum x1, blocking collectives, local(): lax.psum((totals[0], totals[1], attn_bias_full, totals[5], up_bias_full,...  40.8 us
    all_to_all x2, blocking collectives, attn_backward(): lax.all_to_all(grad_triple, 'ctx', split_axis=1, concat_axis=2, tiled=True)  40.7 us
    all_to_all x2, blocking collectives, attn_forward(): lax.all_to_all(triple, 'ctx', split_axis=2, concat_axis=1, tiled=True)  39.9 us
  transfers between devices with their start and end apart: 32, of which 31 were waited for; matrix products, arithmetic and copies ran while one was open for 6% of the time, Pallas kernels for 0%

commit v1 on v0

--- a/solution.py
+++ b/solution.py
@@ -5,6 +5,27 @@
 
 HEAD = 64
 EPSILON = 1e-06
+
+
+def ranges_create(here_x, net_axis):
+    next_value, then, finding = (lax.psum(1, net_axis), lax.axis_index(net_axis), here_x.shape[1])
+    kept_rows = tuple(((dd, (dd + 1) % next_value) for dd in range(next_value)))
+    carry = jnp.zeros((*here_x.shape[:1], next_value * finding, *here_x.shape[2:]), here_x.dtype)
+    carry = lax.dynamic_update_slice_in_dim(carry, here_x, then * finding, axis=1)
+    newest = a_now = here_x
+    main = next_value // 2
+    made = tuple(((dd, (dd - 1) % next_value) for dd in range(next_value)))
+    for pp in [*range(1, main + 1)]:
+        newest = lax.ppermute(newest, net_axis, kept_rows)
+        carry = lax.dynamic_update_slice_in_dim(
+            carry, newest, (then - pp) % next_value * finding, axis=1
+        )
+        if pp < next_value - main:
+            a_now = lax.ppermute(a_now, net_axis, made)
+            carry = lax.dynamic_update_slice_in_dim(
+                carry, a_now, (then + pp) % next_value * finding, axis=1
+            )
+    return carry
 
 
 def layer_norm(rows, gain, shift):
@@ -110,7 +131,7 @@
         ).astype(jnp.float32)
 
     def spread_grads(values):
-        return lax.all_gather(values, "tp", axis=1, tiled=True)
+        return ranges_create(values, "tp")
 
     def sum_grads(values):
         return lax.psum_scatter(

time: 1770 us -> 1730 us (0.977)
  waiting for transfers between devices: 1180 us -> 1020 us
  local copies, waits for them, and re-layouts: 154 us -> 271 us
  blocking collectives: 197 us -> 157 us
  starting transfers between devices: 2.59 us -> 35.2 us
    all_gather x6 -> x0, waiting for transfers between devices: 161 us -> none  [spread_grads(): return lax.all_gather(values, 'tp', axis=1, tiled=True)]
    dynamic_update_slice x0 -> x24, local copies, waits for them, and re-layouts: none -> 81.4 us  [the longest x12 39.1 us: ranges_create(): lax.dynamic_update_slice_in_dim(carry, newest, (then - pp) % next_value *...]
    ppermute x0 -> x18, waiting for transfers between devices: none -> 42.9 us  [the longest x12 42.9 us: ranges_create(): newest = lax.ppermute(newest, net_axis, kept_rows)]
    all_to_all x2 -> x0, blocking collectives: 40.7 us -> none  [attn_backward(): lax.all_to_all(grad_triple, 'ctx', split_axis=1, concat_axis=2, tiled=True)]
    all_to_all x0 -> x2, waiting for transfers between devices: none -> 35.8 us  [attn_backward(): lax.all_to_all(grad_triple, 'ctx', split_axis=1, concat_axis=2, tiled=True)]
    all_gather x2, waiting for transfers between devices: 35.3 us -> 0.01 us  [fetch_weights(): lax.all_gather(up_wide, 'fsdp', axis=0, tiled=True)]
    all_gather x6, waiting for transfers between devices: 192 us -> 162 us  [spread_rows(): return lax.all_gather(values, 'tp', axis=1, tiled=True)]
    ppermute x0 -> x18, local copies, waits for them, and re-layouts: none -> 28.5 us  [the longest x12 19.5 us: ranges_create(): newest = lax.ppermute(newest, net_axis, kept_rows)]
  transfers between devices with their start and end apart: 32 -> 46, of which waited for: 31 -> 31; matrix products, arithmetic and copies ran while one was open for 6% -> 12% of each run, Pallas kernels for 0% -> 0%
where the time goes in v1:
time: 1730 us; the launch traced here: 1720 us
  waiting for transfers between devices  1020 us (59%)
  local copies, waits for them, and re-layouts  271 us (16%)
  blocking collectives  157 us (9%)
  matrix products  106 us (6%)
  other arithmetic  105 us (6%)
  starting transfers between devices  35.2 us (2%)
    while x32, waiting for transfers between devices  600 us
    all_gather x6, waiting for transfers between devices, spread_rows(): return lax.all_gather(values, 'tp', axis=1, tiled=True)  162 us
    reduce_scatter x1, waiting for transfers between devices, local(): lax.psum_scatter(totals[2], ('fsdp', 'ctx'), scatter_dimension=2, tiled=T...  57.6 us
    reduce_scatter x1, waiting for transfers between devices, local(): lax.psum_scatter(up_total, ('fsdp', 'ctx'), scatter_dimension=0, tiled=True)  46.1 us
    ppermute x12, waiting for transfers between devices, ranges_create(): newest = lax.ppermute(newest, net_axis, kept_rows)  42.9 us
    psum x1, blocking collectives, local(): lax.psum((totals[0], totals[1], attn_bias_full, totals[5], up_bias_full,...  40.8 us
    all_to_all x2, blocking collectives, attn_forward(): lax.all_to_all(triple, 'ctx', split_axis=2, concat_axis=1, tiled=True)  39.7 us
    dynamic_update_slice x12, local copies, waits for them, and re-layouts, ranges_create(): lax.dynamic_update_slice_in_dim(carry, newest, (then - pp) % next_value *...  39.1 us
  transfers between devices with their start and end apart: 46, of which 31 were waited for; matrix products, arithmetic and copies ran while one was open for 12% of the time, Pallas kernels for 0%

profile of v1, /device:TPU:0, one launch (start us, length us, event | category | flops | bytes accessed | tf_op | source)
XLA Modules:
  0.0 1723.6 jit_solution(14047569765148558378)
XLA Ops:
  9.5 1515.9 %while.35 = (s32[]{:T(128)}, f32[3,768]{1,0:T(4,128)}, f32[3,768]{1,0:T(4,128)}, f32[2,3,768,192]{2,3,1,0:T(8,128)}, f32[2,2,192]{2,1,0:T(2,128)}, /*index=5*/f3...) while((s32[]{:T(128)}, f32[3,768]{1,0:T(4,128)}, ...), condition=%wide.region_37.38_spmd.clone, body=%wide.region_0.37_spmd.clone.sunk | while | flops 11599428608 | bytes 425757216 | solution.py:294
  16.9 15.1 all_gather.63
  32.1 14.6 all-gather.11.cloned.1.call-done
  46.7 34.4 %all-gather.9.cloned.1.call-done = bf16[4,196,768]{2,0,1:T(4,128)(2,1)} async-done(((bf16[4,49,768]{2,0,1:T(4,128)(2,1)}), bf16[4,196,768]{2,0,1:T(4,128)(2,1)}) %all-gather.9.cloned.1.call-update) | async-done | bytes 1204240 | tf_op jit(solution)/shard_map/while/body/eval_jaxpr/all_gather | solution.py:126
  90.5 54.9 %all-reduce.24.cloned.1.call-done = bf16[4,196,768]{2,0,1:T(4,128)(2,1)} async-done(((bf16[4,196,768]{2,0,1:T(4,128)(2,1)}), bf16[4,196,768]{2,0,1:T(4,128)(2,1)}) %all-reduce.24.cloned.1.call-update) | async-done | bytes 1204240 | tf_op jit(solution)/shard_map/while
  150.2 30.2 %all-gather.13.cloned.1.call-done = bf16[4,196,768]{2,0,1:T(4,128)(2,1)} async-done(((bf16[4,49,768]{2,0,1:T(4,128)(2,1)}), bf16[4,196,768]{2,0,1:T(4,128)(2,1)}) %all-gather.13.cloned.1.call-update) | async-done | bytes 1204240 | tf_op jit(solution)/shard_map/while/body/eval_jaxpr/all_gather | solution.py:126
  187.6 19.9 %all_to_all.116 = bf16[3,4,196,192]{3,1,0,2:T(4,128)(2,1)S(1)} all-to-all(bf16[3,4,196,192]{3,1,0,2:T(4,128)(2,1)} %copy.348), channel_id=1, replica_groups=mesh['fsdp'=2,'ctx'=4,'tp'=4] {'ctx'}, dimensions={2} | all-to-all | bytes 1806336 | tf_op jit(solution)/shard_map/while/body/eval_jaxpr/all_to_all | solution.py:153
  227.8 11.5 all_to_all.117
  243.6 54.7 %all-reduce.26.cloned.1.call-done = bf16[4,196,768]{2,0,1:T(4,128)(2,1)} async-done(((bf16[4,196,768]{2,0,1:T(4,128)(2,1)}), bf16[4,196,768]{2,0,1:T(4,128)(2,1)}) %all-reduce.26.cloned.1.call-update) | async-done | bytes 1204240 | tf_op jit(solution)/shard_map/while
  307.0 8.1 collective-permute-done
  336.6 17.7 %all-gather.15.cloned.1.call-done = bf16[4,196,768]{2,0,1:T(4,128)(2,1)} async-done(((bf16[4,49,768]{2,0,1:T(4,128)(2,1)}), bf16[4,196,768]{2,0,1:T(4,128)(2,1)}) %all-gather.15.cloned.1.call-update) | async-done | bytes 1204240 | tf_op jit(solution)/shard_map/while/body/eval_jaxpr/all_gather | solution.py:126
  359.0 6.8 multiply_convert_fusion.6
  365.8 12.0 all-gather.17.cloned.1.call-done
  377.8 5.6 convert_reduce_fusion.21
  386.2 57.0 %all-reduce.28.cloned.1.call-done = bf16[4,196,768]{2,0,1:T(4,128)(2,1)} async-done(((bf16[4,196,768]{2,0,1:T(4,128)(2,1)}), bf16[4,196,768]{2,0,1:T(4,128)(2,1)}) %all-reduce.28.cloned.1.call-update) | async-done | bytes 1204240 | tf_op jit(solution)/shard_map/while
  455.1 8.3 collective-permute-done.3
  489.8 11.1 all_to_all.118
  531.4 17.9 %all-to-all-done.3 = bf16[3,16,49,192]{3,2,0,1:T(8,128)(2,1)} async-done(((bf16[3,16,49,192]{3,2,0,1:T(8,128)(2,1)}), bf16[3,16,49,192]{3,2,0,1:T(8,128)(2,1)}, u32[]{:S(2)}, u32[]{:S(2)}) %all-to-all-start.3) | async-done | bytes 903200 | tf_op jit(solution)/shard_map/while/body/eval_jaxpr/all_to_all | solution.py:179
  565.8 45.8 %all-reduce.30.cloned.1.call-done = bf16[4,196,768]{2,0,1:T(4,128)(2,1)} async-done(((bf16[4,196,768]{2,0,1:T(4,128)(2,1)}), bf16[4,196,768]{2,0,1:T(4,128)(2,1)}) %all-reduce.30.cloned.1.call-update) | async-done | bytes 1204240 | tf_op jit(solution)/shard_map/while
  628.5 5.0 collective-permute-done.6
  672.4 88.7 %all-reduce.32.cloned.1.call-done = (bf16[4,196,768]{2,0,1:T(4,128)(2,1)}, bf16[4,196,768]{2,0,1:T(4,128)(2,1)}) async-done(((bf16[4,196,768]{2,0,1:T(4,128)(2,1)}, bf16[4,196,768]{2,0,1:T(4,128)(2,1)}), (bf16[4,196,768]{2,0,1:T(4,128)(2,1)}, bf16[4,196,768]{2,0,1:T(4,128)(2,1)})) %all-reduce.32.cloned.1.call-update) | async-done | bytes 2408464 | tf_op jit(solution)/shard_map/while
  774.9 15.7 all_gather.63
  790.6 12.7 all-gather.11.cloned.1.call-done
  803.4 31.9 %all-gather.9.cloned.1.call-done = bf16[4,196,768]{2,0,1:T(4,128)(2,1)} async-done(((bf16[4,49,768]{2,0,1:T(4,128)(2,1)}), bf16[4,196,768]{2,0,1:T(4,128)(2,1)}) %all-gather.9.cloned.1.call-update) | async-done | bytes 1204240 | tf_op jit(solution)/shard_map/while/body/eval_jaxpr/all_gather | solution.py:126
  844.7 54.9 %all-reduce.24.cloned.1.call-done = bf16[4,196,768]{2,0,1:T(4,128)(2,1)} async-done(((bf16[4,196,768]{2,0,1:T(4,128)(2,1)}), bf16[4,196,768]{2,0,1:T(4,128)(2,1)}) %all-reduce.24.cloned.1.call-update) | async-done | bytes 1204240 | tf_op jit(solution)/shard_map/while
  904.5 30.2 %all-gather.13.cloned.1.call-done = bf16[4,196,768]{2,0,1:T(4,128)(2,1)} async-done(((bf16[4,49,768]{2,0,1:T(4,128)(2,1)}), bf16[4,196,768]{2,0,1:T(4,128)(2,1)}) %all-gather.13.cloned.1.call-update) | async-done | bytes 1204240 | tf_op jit(solution)/shard_map/while/body/eval_jaxpr/all_gather | solution.py:126
  941.9 19.8 %all_to_all.116 = bf16[3,4,196,192]{3,1,0,2:T(4,128)(2,1)S(1)} all-to-all(bf16[3,4,196,192]{3,1,0,2:T(4,128)(2,1)} %copy.348), channel_id=1, replica_groups=mesh['fsdp'=2,'ctx'=4,'tp'=4] {'ctx'}, dimensions={2} | all-to-all | bytes 1806336 | tf_op jit(solution)/shard_map/while/body/eval_jaxpr/all_to_all | solution.py:153
  981.9 11.5 all_to_all.117
  997.8 54.7 %all-reduce.26.cloned.1.call-done = bf16[4,196,768]{2,0,1:T(4,128)(2,1)} async-done(((bf16[4,196,768]{2,0,1:T(4,128)(2,1)}), bf16[4,196,768]{2,0,1:T(4,128)(2,1)}) %all-reduce.26.cloned.1.call-update) | async-done | bytes 1204240 | tf_op jit(solution)/shard_map/while
  1061.1 8.1 collective-permute-done
  1090.5 17.7 %all-gather.15.cloned.1.call-done = bf16[4,196,768]{2,0,1:T(4,128)(2,1)} async-done(((bf16[4,49,768]{2,0,1:T(4,128)(2,1)}), bf16[4,196,768]{2,0,1:T(4,128)(2,1)}) %all-gather.15.cloned.1.call-update) | async-done | bytes 1204240 | tf_op jit(solution)/shard_map/while/body/eval_jaxpr/all_gather | solution.py:126
  1113.0 6.8 multiply_convert_fusion.6
  1119.8 12.0 all-gather.17.cloned.1.call-done
  1131.8 5.6 convert_reduce_fusion.21
  1140.1 57.1 %all-reduce.28.cloned.1.call-done = bf16[4,196,768]{2,0,1:T(4,128)(2,1)} async-done(((bf16[4,196,768]{2,0,1:T(4,128)(2,1)}), bf16[4,196,768]{2,0,1:T(4,128)(2,1)}) %all-reduce.28.cloned.1.call-update) | async-done | bytes 1204240 | tf_op jit(solution)/shard_map/while
  1209.1 8.3 collective-permute-done.3
  1243.8 11.1 all_to_all.118
  1280.9 4.4 all-to-all-start.3
  1285.4 17.9 %all-to-all-done.3 = bf16[3,16,49,192]{3,2,0,1:T(8,128)(2,1)} async-done(((bf16[3,16,49,192]{3,2,0,1:T(8,128)(2,1)}), bf16[3,16,49,192]{3,2,0,1:T(8,128)(2,1)}, u32[]{:S(2)}, u32[]{:S(2)}) %all-to-all-start.3) | async-done | bytes 903200 | tf_op jit(solution)/shard_map/while/body/eval_jaxpr/all_to_all | solution.py:179
  1315.1 5.4 bitcast_add_fusion.4
  1322.3 43.3 %all-reduce.30.cloned.1.call-done = bf16[4,196,768]{2,0,1:T(4,128)(2,1)} async-done(((bf16[4,196,768]{2,0,1:T(4,128)(2,1)}), bf16[4,196,768]{2,0,1:T(4,128)(2,1)}) %all-reduce.30.cloned.1.call-update) | async-done | bytes 1204240 | tf_op jit(solution)/shard_map/while
  1382.5 5.0 collective-permute-done.6
  1428.4 86.6 %all-reduce.32.cloned.1.call-done = (bf16[4,196,768]{2,0,1:T(4,128)(2,1)}, bf16[4,196,768]{2,0,1:T(4,128)(2,1)}) async-done(((bf16[4,196,768]{2,0,1:T(4,128)(2,1)}, bf16[4,196,768]{2,0,1:T(4,128)(2,1)}), (bf16[4,196,768]{2,0,1:T(4,128)(2,1)}, bf16[4,196,768]{2,0,1:T(4,128)(2,1)})) %all-reduce.32.cloned.1.call-update) | async-done | bytes 2408464 | tf_op jit(solution)/shard_map/while
  1534.1 5.7 copy.207
  1540.8 40.8 %all-reduce.7 = (f32[3,768]{1,0:T(4,128)}, f32[3,768]{1,0:T(4,128)}, f32[2,2,768]{2,1,0:T(2,128)S(1)}, f32[2,768]{1,0:T(2,128)}, f32[3072]{0:T(1024)}, /*index=5*/f32[768]{0:T(1024)}) all-reduce(f32[3,768]{1,0:T(4,128)S(1)} %copy-done.64, f32[3,768]{1,0:T(4,128)S(1)} %copy-done.67, ...), channel_id=1, replica_groups=mesh['fsdp'=2,'ctx'=4,'tp'=4] {'fsdp','ctx','tp'}, use_global_device_ids=true, to_apply=%region_38.39 | all-reduce | flops 13056 | bytes 104448 | tf_op jit(solution)/shard_map/psum | solution.py:311
  1584.2 27.9 %reduce-scatter.11.cloned.1.call-done = f32[768,96]{0,1:T(8,128)} async-done(((f32[768,768]{0,1:T(8,128)}), f32[768,96]{0,1:T(8,128)}) %reduce-scatter.11.cloned.1.call-update) | async-done | bytes 294928 | tf_op jit(solution)/shard_map/reduce_scatter | solution.py:306
  1612.1 46.1 %reduce-scatter.9.cloned.1.call-done = f32[96,768]{1,0:T(8,128)} async-done(((f32[768,768]{1,0:T(8,128)}), f32[96,768]{1,0:T(8,128)}) %reduce-scatter.9.cloned.1.call-update) | async-done | bytes 294928 | tf_op jit(solution)/shard_map/reduce_scatter | solution.py:305
  1658.2 57.6 %reduce-scatter.7.cloned.1.call-done = f32[2,3,96,192]{3,2,1,0:T(8,128)} async-done(((f32[2,3,768,192]{3,2,1,0:T(8,128)}), f32[2,3,96,192]{3,2,1,0:T(8,128)}) %reduce-scatter.7.cloned.1.call-update) | async-done | bytes 442384 | tf_op jit(solution)/shard_map/reduce_scatter | solution.py:303
  (818 shorter events, 480.6 us)
Async XLA Ops:
  9.5 37.2 %all-gather.11.cloned.1.call-start = ((), (), s32[]{:S(2)}) async-start(), calls=%async_computation.14 | async-start | bytes 2654208 | tf_op jit(solution)/shard_map/while/body/eval_jaxpr/all_gather | solution.py:119
  10.2 70.8 %all-gather.9.cloned.1.call-start = ((), (), s32[]{:S(2)}) async-start(), calls=%async_computation.13 | async-start | bytes 1505280 | tf_op jit(solution)/shard_map/while/body/eval_jaxpr/all_gather | solution.py:126
  12.9 135.2 %copy-start.56 = (f32[768]{0:T(1024)}, f32[768]{0:T(1024)S(1)}, u32[]{:S(2)}) copy-start(f32[768]{0:T(1024)S(1)} %get-tuple-element.834) | copy-start | bytes 9220 | tf_op jit(solution)/shard_map/while
  16.7 128.7 %all-reduce.24.cloned.1.call-start = ((), (), s32[]{:S(2)}) async-start(), calls=%async_computation.15 | async-start | bytes 2408448 | tf_op jit(solution)/shard_map/while
  89.1 91.4 %all-gather.13.cloned.1.call-start = ((), (), s32[]{:S(2)}) async-start(), calls=%async_computation.16 | async-start | bytes 1505280 | tf_op jit(solution)/shard_map/while/body/eval_jaxpr/all_gather | solution.py:126
  150.2 148.2 %all-reduce.26.cloned.1.call-start = ((), (), s32[]{:S(2)}) async-start(), calls=%async_computation.17 | async-start | bytes 2408448 | tf_op jit(solution)/shard_map/while
  243.0 93.6 %all-gather.7.cloned.1.call-start = ((), (), s32[]{:S(2)}) async-start(), calls=%async_computation.12 | async-start | bytes 1769472 | tf_op jit(solution)/shard_map/while/body/eval_jaxpr/all_gather | solution.py:121
  243.6 110.7 %all-gather.15.cloned.1.call-start = ((), (), s32[]{:S(2)}) async-start(), calls=%async_computation.18 | async-start | bytes 1505280 | tf_op jit(solution)/shard_map/while/body/eval_jaxpr/all_gather | solution.py:126
  301.3 76.5 %all-gather.17.cloned.1.call-start = ((), (), s32[]{:S(2)}) async-start(), calls=%async_computation.19 | async-start | bytes 1769472 | tf_op jit(solution)/shard_map/while/body/eval_jaxpr/all_gather | solution.py:122
  303.1 11.9 collective-permute-start
  304.6 21.4 %collective-permute-start.1 = (bf16[4,49,768]{2,0,1:T(4,128)(2,1)S(1)}, bf16[4,49,768]{2,0,1:T(4,128)(2,1)}, u32[]{:S(2)}, u32[]{:S(2)}) collective-permute-start(bf16[4,49,768]{2,0,1:T(4,128)(2,1)S(1)} %get-tuple-element.862), channel_id=1, source_target_pairs={{0,3},{1,0},{2,1},{3,2},{4,7},{5,4},{6,5},{7,6},{8,11},{9,8},{10,9... | collective-permute-start | bytes 903176 | tf_op jit(solution)/shard_map/while/body/eval_jaxpr/ppermute | solution.py:24
  315.1 16.2 collective-permute-start.2
  315.1 128.1 %all-reduce.28.cloned.1.call-start = ((), (), s32[]{:S(2)}) async-start(), calls=%async_computation.20 | async-start | bytes 2408448 | tf_op jit(solution)/shard_map/while
  451.3 12.1 collective-permute-start.3
  452.7 21.9 %collective-permute-start.4 = (bf16[4,49,768]{2,0,1:T(4,128)(2,1)}, bf16[4,49,768]{2,0,1:T(4,128)(2,1)}, u32[]{:S(2)}, u32[]{:S(2)}) collective-permute-start(bf16[4,49,768]{2,0,1:T(4,128)(2,1)} %get-tuple-element.867), channel_id=1, source_target_pairs={{0,3},{1,0},{2,1},{3,2},{4,7},{5,4},{6,5},{7,6},{8,11},{9,8},{10,9... | collective-permute-start | bytes 903176 | tf_op jit(solution)/shard_map/while/body/eval_jaxpr/ppermute | solution.py:24
  463.4 16.5 collective-permute-start.5
  526.9 22.4 %all-to-all-start.3 = ((bf16[3,16,49,192]{3,2,0,1:T(8,128)(2,1)}), bf16[3,16,49,192]{3,2,0,1:T(8,128)(2,1)}, u32[]{:S(2)}, u32[]{:S(2)}) async-start(bf16[3,16,49,192]{3,2,0,1:T(8,128)(2,1)} %copy.371), calls=%async_computation.3 | async-start | bytes 2752512 | tf_op jit(solution)/shard_map/while/body/eval_jaxpr/all_to_all | solution.py:179
  531.3 80.3 %all-reduce.30.cloned.1.call-start = ((), (), s32[]{:S(2)}) async-start(), calls=%async_computation.21 | async-start | bytes 2408448 | tf_op jit(solution)/shard_map/while
  554.0 207.0 %all-reduce.32.cloned.1.call-start = ((), (), s32[]{:S(2)}) async-start(), calls=%async_computation.22 | async-start | bytes 4816896 | tf_op jit(solution)/shard_map/while
  621.4 12.2 collective-permute-start.6
  626.1 17.4 %collective-permute-start.7 = (bf16[4,49,768]{2,0,1:T(4,128)(2,1)}, bf16[4,49,768]{2,0,1:T(4,128)(2,1)}, u32[]{:S(2)}, u32[]{:S(2)}) collective-permute-start(bf16[4,49,768]{2,0,1:T(4,128)(2,1)} %get-tuple-element.873), channel_id=1, source_target_pairs={{0,3},{1,0},{2,1},{3,2},{4,7},{5,4},{6,5},{7,6},{8,11},{9,8},{10,9... | collective-permute-start | bytes 903176 | tf_op jit(solution)/shard_map/while/body/eval_jaxpr/ppermute | solution.py:24
  633.6 14.3 collective-permute-start.8
  767.7 35.7 %all-gather.11.cloned.1.call-start = ((), (), s32[]{:S(2)}) async-start(), calls=%async_computation.14 | async-start | bytes 2654208 | tf_op jit(solution)/shard_map/while/body/eval_jaxpr/all_gather | solution.py:119
  768.3 67.0 %all-gather.9.cloned.1.call-start = ((), (), s32[]{:S(2)}) async-start(), calls=%async_computation.13 | async-start | bytes 1505280 | tf_op jit(solution)/shard_map/while/body/eval_jaxpr/all_gather | solution.py:126
  770.9 131.4 %copy-start.56 = (f32[768]{0:T(1024)}, f32[768]{0:T(1024)S(1)}, u32[]{:S(2)}) copy-start(f32[768]{0:T(1024)S(1)} %get-tuple-element.834) | copy-start | bytes 9220 | tf_op jit(solution)/shard_map/while
  774.8 124.9 %all-reduce.24.cloned.1.call-start = ((), (), s32[]{:S(2)}) async-start(), calls=%async_computation.15 | async-start | bytes 2408448 | tf_op jit(solution)/shard_map/while
  843.4 91.3 %all-gather.13.cloned.1.call-start = ((), (), s32[]{:S(2)}) async-start(), calls=%async_computation.16 | async-start | bytes 1505280 | tf_op jit(solution)/shard_map/while/body/eval_jaxpr/all_gather | solution.py:126
  904.4 148.0 %all-reduce.26.cloned.1.call-start = ((), (), s32[]{:S(2)}) async-start(), calls=%async_computation.17 | async-start | bytes 2408448 | tf_op jit(solution)/shard_map/while
  997.1 93.4 %all-gather.7.cloned.1.call-start = ((), (), s32[]{:S(2)}) async-start(), calls=%async_computation.12 | async-start | bytes 1769472 | tf_op jit(solution)/shard_map/while/body/eval_jaxpr/all_gather | solution.py:121
  997.7 110.5 %all-gather.15.cloned.1.call-start = ((), (), s32[]{:S(2)}) async-start(), calls=%async_computation.18 | async-start | bytes 1505280 | tf_op jit(solution)/shard_map/while/body/eval_jaxpr/all_gather | solution.py:126
  1055.5 76.3 %all-gather.17.cloned.1.call-start = ((), (), s32[]{:S(2)}) async-start(), calls=%async_computation.19 | async-start | bytes 1769472 | tf_op jit(solution)/shard_map/while/body/eval_jaxpr/all_gather | solution.py:122
  1057.3 11.9 collective-permute-start
  1058.7 21.2 %collective-permute-start.1 = (bf16[4,49,768]{2,0,1:T(4,128)(2,1)S(1)}, bf16[4,49,768]{2,0,1:T(4,128)(2,1)}, u32[]{:S(2)}, u32[]{:S(2)}) collective-permute-start(bf16[4,49,768]{2,0,1:T(4,128)(2,1)S(1)} %get-tuple-element.862), channel_id=1, source_target_pairs={{0,3},{1,0},{2,1},{3,2},{4,7},{5,4},{6,5},{7,6},{8,11},{9,8},{10,9... | collective-permute-start | bytes 903176 | tf_op jit(solution)/shard_map/while/body/eval_jaxpr/ppermute | solution.py:24
  1069.2 16.0 collective-permute-start.2
  1069.2 128.0 %all-reduce.28.cloned.1.call-start = ((), (), s32[]{:S(2)}) async-start(), calls=%async_computation.20 | async-start | bytes 2408448 | tf_op jit(solution)/shard_map/while
  1205.3 12.1 collective-permute-start.3
  1206.7 21.9 %collective-permute-start.4 = (bf16[4,49,768]{2,0,1:T(4,128)(2,1)}, bf16[4,49,768]{2,0,1:T(4,128)(2,1)}, u32[]{:S(2)}, u32[]{:S(2)}) collective-permute-start(bf16[4,49,768]{2,0,1:T(4,128)(2,1)} %get-tuple-element.867), channel_id=1, source_target_pairs={{0,3},{1,0},{2,1},{3,2},{4,7},{5,4},{6,5},{7,6},{8,11},{9,8},{10,9... | collective-permute-start | bytes 903176 | tf_op jit(solution)/shard_map/while/body/eval_jaxpr/ppermute | solution.py:24
  1217.4 16.5 collective-permute-start.5
  1280.9 22.4 %all-to-all-start.3 = ((bf16[3,16,49,192]{3,2,0,1:T(8,128)(2,1)}), bf16[3,16,49,192]{3,2,0,1:T(8,128)(2,1)}, u32[]{:S(2)}, u32[]{:S(2)}) async-start(bf16[3,16,49,192]{3,2,0,1:T(8,128)(2,1)} %copy.371), calls=%async_computation.3 | async-start | bytes 2752512 | tf_op jit(solution)/shard_map/while/body/eval_jaxpr/all_to_all | solution.py:179
  1285.3 80.3 %all-reduce.30.cloned.1.call-start = ((), (), s32[]{:S(2)}) async-start(), calls=%async_computation.21 | async-start | bytes 2408448 | tf_op jit(solution)/shard_map/while
  1308.0 207.0 %all-reduce.32.cloned.1.call-start = ((), (), s32[]{:S(2)}) async-start(), calls=%async_computation.22 | async-start | bytes 4816896 | tf_op jit(solution)/shard_map/while
  1375.4 12.2 collective-permute-start.6
  1380.1 17.4 %collective-permute-start.7 = (bf16[4,49,768]{2,0,1:T(4,128)(2,1)}, bf16[4,49,768]{2,0,1:T(4,128)(2,1)}, u32[]{:S(2)}, u32[]{:S(2)}) collective-permute-start(bf16[4,49,768]{2,0,1:T(4,128)(2,1)} %get-tuple-element.873), channel_id=1, source_target_pairs={{0,3},{1,0},{2,1},{3,2},{4,7},{5,4},{6,5},{7,6},{8,11},{9,8},{10,9... | collective-permute-start | bytes 903176 | tf_op jit(solution)/shard_map/while/body/eval_jaxpr/ppermute | solution.py:24
  1387.6 14.3 collective-permute-start.8
  1525.4 56.9 %reduce-scatter.13.cloned.1.call-start = ((), (), s32[]{:S(2)}) async-start(), calls=%async_computation.11 | async-start | bytes 1327104
  1530.2 81.9 %reduce-scatter.11.cloned.1.call-start = ((), (), s32[]{:S(2)}) async-start(), calls=%async_computation.10 | async-start | bytes 2654208 | tf_op jit(solution)/shard_map/reduce_scatter | solution.py:306
  1533.5 124.7 %reduce-scatter.9.cloned.1.call-start = ((), (), s32[]{:S(2)}) async-start(), calls=%async_computation.9 | async-start | bytes 2654208 | tf_op jit(solution)/shard_map/reduce_scatter | solution.py:305
  1534.0 181.7 %reduce-scatter.7.cloned.1.call-start = ((), (), s32[]{:S(2)}) async-start(), calls=%async_computation.8 | async-start | bytes 5308416 | tf_op jit(solution)/shard_map/reduce_scatter | solution.py:303
  (200 other events, 2962.3 us)
Sparse Core Ops, SparseCore 0:
  11.8 34.7 all-gather.10
  48.8 32.1 all-gather.8
  89.3 56.1 all-reduce.23
  150.3 30.1 all-gather.12
  243.1 55.1 all-reduce.25
  299.7 22.2 all-gather.6
  323.6 30.6 all-gather.14
  355.8 21.9 all-gather.16
  386.3 56.8 all-reduce.27
  554.1 57.3 all-reduce.29
  662.9 98.0 all-reduce.31
  769.7 33.5 all-gather.10
  805.5 29.7 all-gather.8
  843.5 56.1 all-reduce.23
  904.6 30.1 all-gather.12
  997.2 55.1 all-reduce.25
  1053.9 22.2 all-gather.6
  1077.5 30.6 all-gather.14
  1109.8 21.9 all-gather.16
  1140.3 56.8 all-reduce.27
  1308.1 57.3 all-reduce.29
  1416.9 98.0 all-reduce.31
Sparse Core Ops, SparseCore 1:
  1530.3 35.7 reduce-scatter.12
  1569.9 42.2 reduce-scatter.10
  1615.9 42.2 reduce-scatter.8
  1662.2 53.5 reduce-scatter.6
